TPU v7x, 32 devices: a whole 2x2x4 slice. The times are simulated.
32 devices in a mesh: row: 8 (over z, core), col: 4 (over y, x).
Axes of the slice: x: 2, y: 2, z: 4, core: 2. Of those that a mesh axis runs over, the one named last changes fastest.
Arguments:
- iterate: bfloat16 [3584, 18432], P('col', 'row'), may hold values from -5.2 to 5.2
Outputs:
- next_iterate: float32 [3584, 18432], P('col', 'row')
All inputs are finite; a program needn't handle non-finite values.
Results may differ from a plain program's by a relative error of at most 0.0032.
Values may be sent and summed in bfloat16 or wider, within the bound.
A program may use at most 128 MiB of HBM per device.

v0:
```python
import jax
import jax.numpy as jnp
from jax import lax
from jax.sharding import PartitionSpec as P

N = 18432
QUINTIC_A = 3.4445
QUINTIC_B = -4.775
QUINTIC_C = 2.0315


def local(iterate):
    inverse = 1.0 / N
    column_slab = lax.all_gather(iterate, "col", axis=0, tiled=True)
    gram_total = lax.psum_scatter(
        lax.dot_general(
            column_slab, iterate, (((1,), (1,)), ((), ())), preferred_element_type=jnp.float32
        ),
        "row",
        scatter_dimension=0,
        tiled=True,
    )
    gram_tile = (gram_total * inverse).astype(jnp.bfloat16)
    row_panel = lax.all_gather(gram_tile, "col", axis=1, tiled=True)
    square = jnp.dot(
        row_panel,
        lax.all_gather(gram_tile, "row", axis=0, tiled=True),
        preferred_element_type=jnp.float32,
    )
    poly_tile = (QUINTIC_B * gram_tile.astype(jnp.float32) + QUINTIC_C * square).astype(
        jnp.bfloat16
    )
    product = lax.dot_general(
        lax.all_gather(poly_tile, "row", axis=0, tiled=True),
        column_slab,
        (((0,), (0,)), ((), ())),
        preferred_element_type=jnp.float32,
    )
    return QUINTIC_A * iterate.astype(jnp.float32) + product


def solution(mesh):
    placed = (P("col", "row"),)
    return jax.shard_map(
        local, mesh=mesh, in_specs=placed, out_specs=P("col", "row"), check_vma=False
    )
```

profile of v0, /device:TPU:0, one launch (start us, length us, event | category | flops | bytes accessed | tf_op | source)
XLA Modules:
  0.0 536.6 jit_solution(12580601077064805445)
XLA Ops:
  6.5 0.0 all-gather.5.cloned.1.call-start
  6.5 0.7 all-gather.5.cloned.1.call-update
  7.3 0.0 reduce-scatter.2.cloned.1.call-start
  7.3 159.9 %all-gather.5.cloned.1.call-done = bf16[3584,2304]{1,0:T(8,128)(2,1)} async-done(((bf16[896,2304]{1,0:T(8,128)(2,1)}), bf16[3584,2304]{1,0:T(8,128)(2,1)}) %all-gather.5.cloned.1.call-update) | async-done | bytes 16515088 | tf_op jit(solution)/shard_map/all_gather | solution.py:14
  167.2 22.9 %fusion = f32[3584,896]{1,0:T(8,128)} fusion(bf16[3584,2304]{1,0:T(8,128)(2,1)} %all-gather.5.cloned.1.call-done, bf16[896,2304]{1,0:T(8,128)(2,1)} %param.1), kind=kOutput, calls=%fused_computation.3 | convolution fusion | flops 14797504512 | bytes 33488896 | tf_op jit(solution)/shard_map/dot_general | solution.py:16
  190.1 0.0 reduce-scatter.2.cloned.1.call-update
  190.1 0.0 all-gather.7.cloned.1.call-start
  190.2 131.8 %reduce-scatter.2.cloned.1.call-done = f32[448,896]{1,0:T(8,128)} async-done(((f32[3584,896]{1,0:T(8,128)}), f32[448,896]{1,0:T(8,128)}) %reduce-scatter.2.cloned.1.call-update) | async-done | bytes 1605648 | tf_op jit(solution)/shard_map/reduce_scatter | solution.py:15
  322.0 2.4 multiply_convert_fusion
  324.4 0.0 all-gather.7.cloned.1.call-update
  324.4 0.0 all-gather.9.cloned.1.call-start
  324.5 0.5 all-gather.9.cloned.1.call-update
  325.0 0.0 all-gather.11.cloned.1.call-start
  325.0 42.4 %all-gather.7.cloned.1.call-done = bf16[448,3584]{1,0:T(8,128)(2,1)} async-done(((bf16[448,896]{1,0:T(8,128)(2,1)}), bf16[448,3584]{1,0:T(8,128)(2,1)}) %all-gather.7.cloned.1.call-update) | async-done | bytes 3211280 | tf_op jit(solution)/shard_map/all_gather | solution.py:24
  367.5 67.4 %all-gather.9.cloned.1.call-done = bf16[3584,896]{1,0:T(8,128)(2,1)} async-done(((bf16[448,896]{1,0:T(8,128)(2,1)}), bf16[3584,896]{1,0:T(8,128)(2,1)}) %all-gather.9.cloned.1.call-update) | async-done | bytes 6422544 | tf_op jit(solution)/shard_map/all_gather | solution.py:27
  434.8 8.3 %add_convert_fusion = bf16[448,896]{1,0:T(8,128)(2,1)} fusion(bf16[448,896]{1,0:T(8,128)(2,1)} %multiply_convert_fusion, bf16[448,3584]{1,0:T(8,128)(2,1)} %all-gather.7.cloned.1.call-done, bf16[3584,896]{1,0:T(8,128)(2,1)} %all-gather.9.cloned.1.call-done), kind=kOutput, calls=%fused_computation.1 | convolution fusion | flops 2879299584 | bytes 11239424 | tf_op jit(solution)/shard_map/dot_general | solution.py:25
  443.1 0.0 all-gather.11.cloned.1.call-update
  443.1 64.6 %all-gather.11.cloned.1.call-done = bf16[3584,896]{1,0:T(8,128)(2,1)} async-done(((bf16[448,896]{1,0:T(8,128)(2,1)}), bf16[3584,896]{1,0:T(8,128)(2,1)}) %all-gather.11.cloned.1.call-update) | async-done | bytes 6422544 | tf_op jit(solution)/shard_map/all_gather | solution.py:34
  507.8 22.3 %multiply_add_fusion = f32[896,2304]{1,0:T(8,128)} fusion(bf16[896,2304]{1,0:T(8,128)(2,1)} %param.1, bf16[3584,896]{1,0:T(8,128)(2,1)} %all-gather.11.cloned.1.call-done, bf16[3584,2304]{1,0:T(8,128)(2,1)} %all-gather.5.cloned.1.call-done), kind=kOutput, calls=%fused_computation | convolution fusion | flops 14803697664 | bytes 35323904 | tf_op jit(solution)/shard_map/dot_general | solution.py:33
Async XLA Ops:
  6.5 160.6 %all-gather.5.cloned.1.call-start = ((), (), s32[]{:S(2)}) async-start(), calls=%async_computation.1 | async-start | bytes 20643840 | tf_op jit(solution)/shard_map/all_gather | solution.py:14
  7.3 314.7 %reduce-scatter.2.cloned.1.call-start = ((), (), s32[]{:S(2)}) async-start(), calls=%async_computation.2 | async-start | bytes 14450688 | tf_op jit(solution)/shard_map/reduce_scatter | solution.py:15
  190.1 177.4 %all-gather.7.cloned.1.call-start = ((), (), s32[]{:S(2)}) async-start(), calls=%async_computation.3 | async-start | bytes 4014080 | tf_op jit(solution)/shard_map/all_gather | solution.py:24
  324.4 110.4 %all-gather.9.cloned.1.call-start = ((), (), s32[]{:S(2)}) async-start(), calls=%async_computation.4 | async-start | bytes 7225344 | tf_op jit(solution)/shard_map/all_gather | solution.py:27
  325.0 182.8 %all-gather.11.cloned.1.call-start = ((), (), s32[]{:S(2)}) async-start(), calls=%async_computation.5 | async-start | bytes 7225344 | tf_op jit(solution)/shard_map/all_gather | solution.py:34
Sparse Core Ops, SparseCore 0:
  9.2 157.9 all-gather.4
  190.2 131.6 reduce-scatter.1
  324.5 42.8 all-gather.6
  369.0 65.8 all-gather.8
  443.2 64.4 all-gather.10
where the time goes:
time: 537 us
  waiting for transfers between devices  467 us (87%)
  matrix products  53.4 us (10%)
  between operations  13.1 us (2%)
    all_gather x1, waiting for transfers between devices, local(): column_slab = lax.all_gather(iterate, 'col', axis=0, tiled=True)  160 us
    reduce_scatter x1, waiting for transfers between devices, local(): lax.psum_scatter(lax.dot_general(column_slab, iterate, (((1,), (1,)), (()...  132 us
    all_gather x1, waiting for transfers between devices, local(): lax.all_gather(gram_tile, 'row', axis=0, tiled=True)  67.4 us
    all_gather x1, waiting for transfers between devices, local(): lax.all_gather(poly_tile, 'row', axis=0, tiled=True)  64.6 us
    all_gather x1, waiting for transfers between devices, local(): row_panel = lax.all_gather(gram_tile, 'col', axis=1, tiled=True)  42.4 us
    dot_general x1, matrix products, local(): lax.dot_general(column_slab, iterate, (((1,), (1,)), ((), ())), preferred...  22.9 us
    dot_general x1, matrix products, local(): lax.dot_general(lax.all_gather(poly_tile, 'row', axis=0, tiled=True), col...  22.3 us
  transfers between devices with their start and end apart: 5, of which 5 were waited for; matrix products, arithmetic and copies ran while one was open for 0% of the time, Pallas kernels for 0%

commit v1 on v0

--- a/solution.py
+++ b/solution.py
@@ -7,6 +7,19 @@
 QUINTIC_A = 3.4445
 QUINTIC_B = -4.775
 QUINTIC_C = 2.0315
+
+
+def collect(shard, axis, dim):
+    ways = lax.axis_size(axis)
+    up = [(d, (d + 1) % ways) for d in range(ways)]
+    down = [(d, (d - 1) % ways) for d in range(ways)]
+    earlier, later = ([shard], [shard])
+    for _ in range(ways // 2):
+        earlier.append(lax.ppermute(earlier[-1], axis, up))
+    for _ in range((ways - 1) // 2):
+        later.append(lax.ppermute(later[-1], axis, down))
+    line = jnp.concatenate([*earlier[::-1], *later[1:]], axis=dim)
+    return jnp.roll(line, (lax.axis_index(axis) - ways // 2) * shard.shape[dim], axis=dim)
 
 
 def local(iterate):
@@ -21,7 +34,7 @@
         tiled=True,
     )
     gram_tile = (gram_total * inverse).astype(jnp.bfloat16)
-    row_panel = lax.all_gather(gram_tile, "col", axis=1, tiled=True)
+    row_panel = collect(gram_tile, "col", 1)
     square = jnp.dot(
         row_panel,
         lax.all_gather(gram_tile, "row", axis=0, tiled=True),

time: 537 us -> 492 us (0.916)
  waiting for transfers between devices: 467 us -> 405 us
  local copies, waits for them, and re-layouts: 0 us -> 10.1 us
    all_gather x1, waiting for transfers between devices: 67.4 us -> 2.52 us  [local(): lax.all_gather(gram_tile, 'row', axis=0, tiled=True)]
    ppermute x0 -> x3, waiting for transfers between devices: none -> 45.2 us  [the longest x2 35.9 us: collect(): earlier.append(lax.ppermute(earlier[-1], axis, up))]
    all_gather x1 -> x0, waiting for transfers between devices: 42.4 us -> none  [local(): row_panel = lax.all_gather(gram_tile, 'col', axis=1, tiled=True)]
    unnamed x0 -> x11, local copies, waits for them, and re-layouts: none -> 8.03 us
  transfers between devices with their start and end apart: 5 -> 7, of which waited for: 5 -> 7; matrix products, arithmetic and copies ran while one was open for 0% -> 2% of each run, Pallas kernels for 0% -> 0%
where the time goes in v1:
time: 492 us; the launch traced here: 491 us
  waiting for transfers between devices  405 us (82%)
  matrix products  53.5 us (11%)
  between operations  13.1 us (3%)
  local copies, waits for them, and re-layouts  10.1 us (2%)
    all_gather x1, waiting for transfers between devices, local(): column_slab = lax.all_gather(iterate, 'col', axis=0, tiled=True)  160 us
    reduce_scatter x1, waiting for transfers between devices, local(): lax.psum_scatter(lax.dot_general(column_slab, iterate, (((1,), (1,)), (()...  132 us
    all_gather x1, waiting for transfers between devices, local(): lax.all_gather(poly_tile, 'row', axis=0, tiled=True)  65.4 us
    ppermute x2, waiting for transfers between devices, collect(): earlier.append(lax.ppermute(earlier[-1], axis, up))  35.9 us
    dot_general x1, matrix products, local(): lax.dot_general(column_slab, iterate, (((1,), (1,)), ((), ())), preferred...  22.9 us
    dot_general x1, matrix products, local(): lax.dot_general(lax.all_gather(poly_tile, 'row', axis=0, tiled=True), col...  22.3 us
  transfers between devices with their start and end apart: 7, of which 7 were waited for; matrix products, arithmetic and copies ran while one was open for 2% of the time, Pallas kernels for 0%

profile of v1, /device:TPU:0, one launch (start us, length us, event | category | flops | bytes accessed | tf_op | source)
XLA Modules:
  0.0 491.4 jit_solution(9048245141242431785)
XLA Ops:
  6.5 0.0 all-gather.4.cloned.1.call-start
  6.5 0.7 all-gather.4.cloned.1.call-update
  7.3 0.0 reduce-scatter.2.cloned.1.call-start
  7.3 159.9 %all-gather.4.cloned.1.call-done = bf16[3584,2304]{1,0:T(8,128)(2,1)} async-done(((bf16[896,2304]{1,0:T(8,128)(2,1)}), bf16[3584,2304]{1,0:T(8,128)(2,1)}) %all-gather.4.cloned.1.call-update) | async-done | bytes 16515088 | tf_op jit(solution)/shard_map/all_gather | solution.py:27
  167.2 22.9 %fusion.5 = f32[3584,896]{1,0:T(8,128)} fusion(bf16[3584,2304]{1,0:T(8,128)(2,1)} %all-gather.4.cloned.1.call-done, bf16[896,2304]{1,0:T(8,128)(2,1)} %param.1), kind=kOutput, calls=%fused_computation.14 | convolution fusion | flops 14797504512 | bytes 33488896 | tf_op jit(solution)/shard_map/dot_general | solution.py:29
  190.1 0.0 reduce-scatter.2.cloned.1.call-update
  190.1 0.0 all-gather.6.cloned.1.call-start
  190.2 131.8 %reduce-scatter.2.cloned.1.call-done = f32[448,896]{1,0:T(8,128)} async-done(((f32[3584,896]{1,0:T(8,128)}), f32[448,896]{1,0:T(8,128)}) %reduce-scatter.2.cloned.1.call-update) | async-done | bytes 1605648 | tf_op jit(solution)/shard_map/reduce_scatter | solution.py:28
  322.0 2.6 multiply_convert_fusion
  324.5 0.0 all-gather.6.cloned.1.call-update
  324.6 0.0 all-gather.8.cloned.1.call-start
  324.6 1.5 collective-permute-start
  326.1 17.1 %collective-permute-done = bf16[448,896]{1,0:T(8,128)(2,1)S(1)} collective-permute-done((bf16[448,896]{1,0:T(8,128)(2,1)}, bf16[448,896]{1,0:T(8,128)(2,1)S(1)}, u32[]{:S(2)}, u32[]{:S(2)}) %collective-permute-start) | collective-permute-done | bytes 802848 | tf_op jit(solution)/shard_map/ppermute | solution.py:18
  343.3 1.0 collective-permute-start.1
  344.3 1.9 collective-permute-start.2
  346.2 18.8 %collective-permute-done.1 = bf16[448,896]{1,0:T(8,128)(2,1)S(1)} collective-permute-done((bf16[448,896]{1,0:T(8,128)(2,1)S(1)}, bf16[448,896]{1,0:T(8,128)(2,1)S(1)}, u32[]{:S(2)}, u32[]{:S(2)}) %collective-permute-start.1) | collective-permute-done | bytes 802848 | tf_op jit(solution)/shard_map/ppermute | solution.py:18
  365.0 1.0 copy-done.2
  366.0 0.9 constant_dynamic-update-slice_fusion.7
  367.0 0.9 constant_dynamic-update-slice_fusion.6
  367.9 0.0 copy-done
  367.9 1.0 constant_dynamic-update-slice_fusion.5
  368.9 9.2 %collective-permute-done.2 = bf16[448,896]{1,0:T(8,128)(2,1)} collective-permute-done((bf16[448,896]{1,0:T(8,128)(2,1)}, bf16[448,896]{1,0:T(8,128)(2,1)}, u32[]{:S(2)}, u32[]{:S(2)}) %collective-permute-start.2) | collective-permute-done | bytes 802848 | tf_op jit(solution)/shard_map/ppermute | solution.py:20
  378.2 2.1 constant_dynamic-update-slice_fusion.4
  380.3 2.1 constant_dynamic-update-slice_fusion.3
  382.3 0.9 constant_dynamic-update-slice_fusion.2
  383.3 1.0 constant_dynamic-update-slice_fusion.1
  384.3 2.1 constant_dynamic-update-slice_fusion
  386.4 2.5 all-gather.6.cloned.1.call-done
  388.9 8.3 %add_convert_fusion = bf16[448,896]{1,0:T(8,128)(2,1)} fusion(bf16[448,896]{1,0:T(8,128)(2,1)S(1)} %copy-done.1, bf16[3584,896]{1,0:T(8,128)(2,1)} %all-gather.6.cloned.1.call-done, bf16[448,7168]{1,0:T(8,128)(2,1)} %constant_dynamic-update-slice_fusion, s32[]{:T(128)S(6)} %select_n.14), kind=kOutput, calls=%fused_computation.3 | convolution fusion | flops 2879299584 | bytes 11239428 | tf_op jit(solution)/shard_map/dot_general | solution.py:38
  397.2 0.0 all-gather.8.cloned.1.call-update
  397.2 65.4 %all-gather.8.cloned.1.call-done = bf16[3584,896]{1,0:T(8,128)(2,1)} async-done(((bf16[448,896]{1,0:T(8,128)(2,1)}), bf16[3584,896]{1,0:T(8,128)(2,1)}) %all-gather.8.cloned.1.call-update) | async-done | bytes 6422544 | tf_op jit(solution)/shard_map/all_gather | solution.py:47
  462.6 22.3 %multiply_add_fusion = f32[896,2304]{1,0:T(8,128)} fusion(bf16[896,2304]{1,0:T(8,128)(2,1)} %param.1, bf16[3584,896]{1,0:T(8,128)(2,1)} %all-gather.8.cloned.1.call-done, bf16[3584,2304]{1,0:T(8,128)(2,1)} %all-gather.4.cloned.1.call-done), kind=kOutput, calls=%fused_computation | convolution fusion | flops 14803697664 | bytes 35323904 | tf_op jit(solution)/shard_map/dot_general | solution.py:46
  (4 shorter events, 0.0 us)
Async XLA Ops:
  6.5 160.6 %all-gather.4.cloned.1.call-start = ((), (), s32[]{:S(2)}) async-start(), calls=%async_computation.1 | async-start | bytes 20643840 | tf_op jit(solution)/shard_map/all_gather | solution.py:27
  7.3 314.7 %reduce-scatter.2.cloned.1.call-start = ((), (), s32[]{:S(2)}) async-start(), calls=%async_computation.2 | async-start | bytes 14450688 | tf_op jit(solution)/shard_map/reduce_scatter | solution.py:28
  190.1 198.8 %all-gather.6.cloned.1.call-start = ((), (), s32[]{:S(2)}) async-start(), calls=%async_computation.3 | async-start | bytes 7225344 | tf_op jit(solution)/shard_map/all_gather | solution.py:40
  322.0 46.0 %copy-start = (f32[448,896]{1,0:T(8,128)S(1)}, f32[448,896]{1,0:T(8,128)}, u32[]{:S(2)}) copy-start(f32[448,896]{1,0:T(8,128)} %reduce-scatter.2.cloned.1.call-done) | copy-start | bytes 4816900
  324.6 138.0 %all-gather.8.cloned.1.call-start = ((), (), s32[]{:S(2)}) async-start(), calls=%async_computation.4 | async-start | bytes 7225344 | tf_op jit(solution)/shard_map/all_gather | solution.py:47
  324.6 18.7 %collective-permute-start = (bf16[448,896]{1,0:T(8,128)(2,1)}, bf16[448,896]{1,0:T(8,128)(2,1)S(1)}, u32[]{:S(2)}, u32[]{:S(2)}) collective-permute-start(bf16[448,896]{1,0:T(8,128)(2,1)} %multiply_convert_fusion), channel_id=1, source_target_pairs={{0,1},{1,2},{2,3},{3,0},{4,5},{5,6},{6,7},{7,4},{8,9},{9,10},{10,1... | collective-permute-start | bytes 2408456 | tf_op jit(solution)/shard_map/ppermute | solution.py:18
  343.3 21.7 %collective-permute-start.1 = (bf16[448,896]{1,0:T(8,128)(2,1)S(1)}, bf16[448,896]{1,0:T(8,128)(2,1)S(1)}, u32[]{:S(2)}, u32[]{:S(2)}) collective-permute-start(bf16[448,896]{1,0:T(8,128)(2,1)S(1)} %collective-permute-done), channel_id=1, source_target_pairs={{0,1},{1,2},{2,3},{3,0},{4,5},{5,6},{6,7},{7,4},{8,9},{9,10},{10,1... | collective-permute-start | bytes 2408456 | tf_op jit(solution)/shard_map/ppermute | solution.py:18
  344.3 33.9 %collective-permute-start.2 = (bf16[448,896]{1,0:T(8,128)(2,1)}, bf16[448,896]{1,0:T(8,128)(2,1)}, u32[]{:S(2)}, u32[]{:S(2)}) collective-permute-start(bf16[448,896]{1,0:T(8,128)(2,1)} %multiply_convert_fusion), channel_id=1, source_target_pairs={{0,3},{1,0},{2,1},{3,2},{4,7},{5,4},{6,5},{7,6},{8,11},{9,8},{10,9... | collective-permute-start | bytes 2408456 | tf_op jit(solution)/shard_map/ppermute | solution.py:20
  365.0 1.0 copy-start.2
  367.0 22.0 %copy-start.1 = (bf16[448,896]{1,0:T(8,128)(2,1)S(1)}, bf16[448,896]{1,0:T(8,128)(2,1)}, u32[]{:S(2)}) copy-start(bf16[448,896]{1,0:T(8,128)(2,1)} %multiply_convert_fusion) | copy-start | bytes 2408452
Sparse Core Ops, SparseCore 0:
  9.2 157.9 all-gather.3
  190.2 131.6 reduce-scatter.1
  324.7 64.1 all-gather.5
  397.3 65.1 all-gather.7
